TPU v7x, 32 devices: a whole 2x2x4 slice. The times are simulated.
32 devices in a mesh: row: 16 (over z, y, x), col: 2 (over core).
Axes of the slice: x: 2, y: 2, z: 4, core: 2. Of those that a mesh axis runs over, the one named last changes fastest.
Arguments:
- features: bfloat16 [8192, 128], P(('row', 'col')), may hold values from -6 to 6
- weight: bfloat16 [128, 256], replicated, may hold values from -0.5 to 0.5
- bias: float32 [256], replicated, may hold values from -3 to 3
- grad_out: bfloat16 [8192, 256], P(('row', 'col')), may hold values from -6 to 6
- tiles: bfloat16 [32, 128, 128, 128], P(('row', 'col')), may hold values from -0.25 to 0.25
- tile_count: int32 [32], P(('row', 'col')), may hold values from 1 to 128, as said below
- tile_dst: int32 [32, 128], P(('row', 'col')), may hold values from 0 to 3
- tile_src: int32 [32, 128], P(('row', 'col')), may hold values from 0 to 9
Outputs:
- activations: bfloat16 [8192, 256], P(('row', 'col'))
- grad_features: bfloat16 [8192, 128], P(('row', 'col'))
- grad_weight: float32 [128, 256], replicated
- grad_bias: float32 [256], replicated
Inputs may be any that keep to these rules, and one draw needn't show every extreme that they name: Slots from tile_count on are ignored; some device holds 128 live slots.
All inputs are finite; a program needn't handle non-finite values.
Results may differ from a plain program's by a relative error of at most 0.019.
Values may be sent and summed in bfloat16 or wider, within the bound.
A program may use at most 64 MiB of HBM per device.

v0:
```python
import math
import jax
import jax.numpy as jnp
from jax import lax
from jax.sharding import PartitionSpec as P


def shifted(value, axis, steps):
    count = lax.axis_size(axis)
    pairs = [(source, (source + steps) % count) for source in range(count)]
    return lax.ppermute(value, axis, pairs)


def local(features, weight, bias, grad_out, tiles, tile_count, tile_dst, tile_src):
    node_dev = features.shape[0]
    in_width = features.shape[1]
    tile = tiles.shape[2]
    maxt = tiles.shape[1]
    band = 2
    tiles_dev = node_dev // tile
    n_col = lax.axis_size("col")
    dst_tiles = n_col * tiles_dev
    window_tiles = (2 * band + 1) * tiles_dev
    nodes_all = node_dev * lax.axis_size("row") * n_col
    group = math.gcd(16, maxt)
    pieces = {0: features}
    for offset in (-2, -1, 1, 2):
        pieces[offset] = shifted(features, "row", -offset)
    window = jnp.concatenate([pieces[o] for o in range(-band, band + 1)], 0).reshape(
        window_tiles, tile, in_width
    )
    tile_local = tiles[0]
    count = tile_count[0]
    dst_local = tile_dst[0]
    src_local = tile_src[0]
    turns = (count + group - 1) // group
    offsets_in = jnp.arange(group, dtype=jnp.int32)

    def forward_step(index, acc):
        start = index * group
        tile_block = lax.dynamic_slice_in_dim(tile_local, start, group, 0)
        src_block = lax.dynamic_slice_in_dim(src_local, start, group, 0)
        dst_block = lax.dynamic_slice_in_dim(dst_local, start, group, 0)
        live = (start + offsets_in < count).astype(jnp.float32)
        prod = jnp.einsum(
            "kij,kjh->kih", tile_block, window[src_block], preferred_element_type=jnp.float32
        )
        return acc.at[dst_block].add(prod * live[:, None, None])

    acc = lax.fori_loop(0, turns, forward_step, jnp.zeros((dst_tiles, tile, in_width), jnp.float32))
    summed = lax.psum_scatter(
        acc.reshape(dst_tiles * tile, in_width).astype(jnp.bfloat16),
        "col",
        scatter_dimension=0,
        tiled=True,
    )
    pre = jnp.dot(summed, weight, preferred_element_type=jnp.float32) + bias
    sig = jax.nn.sigmoid(pre)
    activations = (pre * sig).astype(jnp.bfloat16)
    dpre = (grad_out.astype(jnp.float32) * sig * (1.0 + pre * (1.0 - sig))).astype(jnp.bfloat16)
    grad_agg = lax.dot_general(
        dpre, weight, (((1,), (1,)), ((), ())), preferred_element_type=jnp.float32
    ).astype(jnp.bfloat16)
    block_grads = lax.all_gather(grad_agg, "col", axis=0, tiled=True).reshape(
        dst_tiles, tile, in_width
    )

    def back_step(index, acc_back):
        start = index * group
        tile_block = lax.dynamic_slice_in_dim(tile_local, start, group, 0)
        src_block = lax.dynamic_slice_in_dim(src_local, start, group, 0)
        dst_block = lax.dynamic_slice_in_dim(dst_local, start, group, 0)
        live = (start + offsets_in < count).astype(jnp.float32)
        contrib = jnp.einsum(
            "kji,kjh->kih", tile_block, block_grads[dst_block], preferred_element_type=jnp.float32
        )
        return acc_back.at[src_block].add(contrib * live[:, None, None])

    backs = lax.fori_loop(
        0, turns, back_step, jnp.zeros((window_tiles, tile, in_width), jnp.float32)
    )
    backs = backs.reshape(2 * band + 1, node_dev, in_width)
    total = backs[band]
    for offset in (-2, -1, 1, 2):
        total = total + shifted(backs[offset + band], "row", offset)
    grad_features = total.astype(jnp.bfloat16)
    weight_term = lax.dot_general(
        summed, dpre, (((0,), (0,)), ((), ())), preferred_element_type=jnp.float32
    )
    bias_term = jnp.sum(dpre.astype(jnp.float32), 0)
    weight_total, bias_total = lax.psum((weight_term, bias_term), ("row", "col"))
    scale = math.sqrt(nodes_all)
    grad_weight = weight_total / scale
    grad_bias = bias_total / scale
    return (activations, grad_features, grad_weight, grad_bias)


def solution(mesh):
    in_specs = (
        P(("row", "col"), None),
        P(),
        P(),
        P(("row", "col"), None),
        P(("row", "col"), None, None, None),
        P(("row", "col")),
        P(("row", "col"), None),
        P(("row", "col"), None),
    )
    out_specs = (P(("row", "col"), None), P(("row", "col"), None), P(), P())
    return jax.shard_map(local, mesh=mesh, in_specs=in_specs, out_specs=out_specs, check_vma=False)
```

profile of v0, /device:TPU:0, one launch (start us, length us, event | category | flops | bytes accessed | tf_op | source)
XLA Modules:
  0.0 245.5 jit_solution(1033797611451873253)
XLA Ops:
  7.2 3.0 %collective-permute-start = (bf16[256,128]{1,0:T(8,128)(2,1)}, bf16[256,128]{1,0:T(8,128)(2,1)S(1)}, u32[]{:S(2)}, u32[]{:S(2)}) collective-permute-start(bf16[256,128]{1,0:T(8,128)(2,1)} %param.12), channel_id=1, source_target_pairs={{0,4},{2,6},{4,8},{6,10},{8,12},{10,14},{12,16},{14,18},{16,20},{1... | collective-permute-start | bytes 196616 | tf_op jit(solution)/shard_map/ppermute | solution.py:11
  10.3 4.1 %collective-permute-start.2 = (bf16[256,128]{1,0:T(8,128)(2,1)}, bf16[256,128]{1,0:T(8,128)(2,1)S(1)}, u32[]{:S(2)}, u32[]{:S(2)}) collective-permute-start(bf16[256,128]{1,0:T(8,128)(2,1)} %param.12), channel_id=1, source_target_pairs={{0,30},{2,0},{4,2},{6,4},{8,6},{10,8},{12,10},{14,12},{16,14},{18,... | collective-permute-start | bytes 196616 | tf_op jit(solution)/shard_map/ppermute | solution.py:11
  14.4 1.9 collective-permute-start.3
  17.0 5.5 %collective-permute-done.1 = bf16[256,128]{1,0:T(8,128)(2,1)S(1)} collective-permute-done((bf16[256,128]{1,0:T(8,128)(2,1)}, bf16[256,128]{1,0:T(8,128)(2,1)S(1)}, u32[]{:S(2)}, u32[]{:S(2)}) %collective-permute-start.1) | collective-permute-done | bytes 65568 | tf_op jit(solution)/shard_map/ppermute | solution.py:11
  23.4 20.2 %while.22 = (s32[]{:T(128)}, f32[4,128,128]{2,1,0:T(8,128)S(1)}, s32[]{:T(128)}, s32[128]{0:T(128)}, bf16[128,128,128]{2,1,0:T(8,128)(2,1)}, /*index=5*/s32[128]...) while((s32[]{:T(128)}, f32[4,128,128]{2,1,0:T(8,128)S(1)}, ...), condition=%wide.region_2.3_spmd.clone, body=%wide.region_0.2_spmd.clone.sunk | while | flops 67634328 | bytes 6296307 | solution.py:50
  26.9 1.6 scatter_fusion
  31.9 1.6 scatter_fusion
  37.0 1.6 scatter_fusion
  42.0 1.6 scatter_fusion
  44.4 6.4 %copy.12 = bf16[1,128,128,128]{2,3,1,0:T(8,128)(2,1)} copy(bf16[1,128,128,128]{3,2,1,0:T(8,128)(2,1)} %bitcast.38) | data formatting | bytes 8388608 | tf_op args[4]
  50.9 16.9 %reduce-scatter.2.cloned.1.call-done = bf16[256,128]{1,0:T(8,128)(2,1)} async-done(((bf16[512,128]{1,0:T(8,128)(2,1)}), bf16[256,128]{1,0:T(8,128)(2,1)}) %reduce-scatter.2.cloned.1.call-update) | async-done | bytes 65552 | tf_op jit(solution)/shard_map/reduce_scatter | solution.py:51
  67.8 1.8 convert_reduce_fusion
  69.5 40.4 %psum.15 = f32[256]{0:T(256)S(1)} all-reduce(f32[256]{0:T(256)S(1)} %get-tuple-element.180), channel_id=1, replica_groups=mesh['row'=16,'col'=2] {'row','col'}, use_global_device_ids=true, to_apply=%region_9.10 | all-reduce | flops 256 | bytes 2048 | tf_op jit(solution)/shard_map/psum | solution.py:91
  110.1 1.7 fusion.13
  111.8 1.9 all_gather.3
  113.8 17.5 %while.23 = (s32[]{:T(128)}, f32[10,128,128]{2,1,0:T(8,128)S(1)}, s32[]{:T(128)}, s32[128]{0:T(128)S(1)}, bf16[128,128,128]{1,2,0:T(8,128)(2,1)}, /*index=5*/s32...) while((s32[]{:T(128)}, f32[10,128,128]{2,1,0:T(8,128)S(1)}, ...), condition=%wide.region_6.7_spmd.clone, body=%wide.region_4.6_spmd.clone.sunk | while | flops 67634328 | bytes 6296307 | solution.py:79
  116.6 1.6 scatter_fusion.1
  120.9 1.6 scatter_fusion.1
  125.3 1.6 scatter_fusion.1
  129.7 1.6 scatter_fusion.1
  131.9 5.6 %collective-permute-start.5 = (f32[256,128]{1,0:T(8,128)S(1)}, f32[256,128]{1,0:T(8,128)S(1)}, u32[]{:S(2)}, u32[]{:S(2)}) collective-permute-start(f32[256,128]{1,0:T(8,128)S(1)} %bitcast.43), channel_id=1, source_target_pairs={{0,30},{2,0},{4,2},{6,4},{8,6},{10,8},{12,10},{14,12},{16,14},{18,... | collective-permute-start | bytes 393224 | tf_op jit(solution)/shard_map/ppermute | solution.py:11
  137.6 17.3 %collective-permute-start.4 = (f32[256,128]{1,0:T(8,128)S(1)}, f32[256,128]{1,0:T(8,128)S(1)}, u32[]{:S(2)}, u32[]{:S(2)}) collective-permute-start(f32[256,128]{1,0:T(8,128)S(1)} %bitcast.42), channel_id=1, source_target_pairs={{0,28},{2,30},{4,0},{6,2},{8,4},{10,6},{12,8},{14,10},{16,12},{18,... | collective-permute-start | bytes 393224 | tf_op jit(solution)/shard_map/ppermute | solution.py:11
  154.9 81.5 %all-reduce.2.cloned.1.call-done = f32[128,256]{1,0:T(8,128)} async-done(((f32[128,256]{1,0:T(8,128)}), f32[128,256]{1,0:T(8,128)}) %all-reduce.2.cloned.1.call-update) | async-done | bytes 131088 | tf_op jit(solution)/shard_map/psum | solution.py:91
  236.4 1.6 broadcast_multiply_fusion
  (76 shorter events, 27.8 us)
Async XLA Ops:
  7.2 60.6 %copy-start = (bf16[128,256]{1,0:T(8,128)(2,1)S(1)}, bf16[128,256]{1,0:T(8,128)(2,1)}, u32[]{:S(2)}) copy-start(bf16[128,256]{1,0:T(8,128)(2,1)} %param.13) | copy-start | bytes 196612
  7.2 60.6 %reduce-scatter.2.cloned.1.call-start = ((), (), s32[]{:S(2)}) async-start(), calls=%async_computation.1 | async-start | bytes 196608 | tf_op jit(solution)/shard_map/reduce_scatter | solution.py:51
  7.2 9.7 %collective-permute-start = (bf16[256,128]{1,0:T(8,128)(2,1)}, bf16[256,128]{1,0:T(8,128)(2,1)S(1)}, u32[]{:S(2)}, u32[]{:S(2)}) collective-permute-start(bf16[256,128]{1,0:T(8,128)(2,1)} %param.12), channel_id=1, source_target_pairs={{0,4},{2,6},{4,8},{6,10},{8,12},{10,14},{12,16},{14,18},{16,20},{1... | collective-permute-start | bytes 196616 | tf_op jit(solution)/shard_map/ppermute | solution.py:11
  10.3 13.1 %collective-permute-start.2 = (bf16[256,128]{1,0:T(8,128)(2,1)}, bf16[256,128]{1,0:T(8,128)(2,1)S(1)}, u32[]{:S(2)}, u32[]{:S(2)}) collective-permute-start(bf16[256,128]{1,0:T(8,128)(2,1)} %param.12), channel_id=1, source_target_pairs={{0,30},{2,0},{4,2},{6,4},{8,6},{10,8},{12,10},{14,12},{16,14},{18,... | collective-permute-start | bytes 196616 | tf_op jit(solution)/shard_map/ppermute | solution.py:11
  14.4 8.1 %collective-permute-start.1 = (bf16[256,128]{1,0:T(8,128)(2,1)}, bf16[256,128]{1,0:T(8,128)(2,1)S(1)}, u32[]{:S(2)}, u32[]{:S(2)}) collective-permute-start(bf16[256,128]{1,0:T(8,128)(2,1)} %param.12), channel_id=1, source_target_pairs={{0,2},{2,4},{4,6},{6,8},{8,10},{10,12},{12,14},{14,16},{16,18},{18... | collective-permute-start | bytes 196616 | tf_op jit(solution)/shard_map/ppermute | solution.py:11
  14.4 9.0 %collective-permute-start.3 = (bf16[256,128]{1,0:T(8,128)(2,1)}, bf16[256,128]{1,0:T(8,128)(2,1)S(1)}, u32[]{:S(2)}, u32[]{:S(2)}) collective-permute-start(bf16[256,128]{1,0:T(8,128)(2,1)} %param.12), channel_id=1, source_target_pairs={{0,28},{2,30},{4,0},{6,2},{8,4},{10,6},{12,8},{14,10},{16,12},{18,... | collective-permute-start | bytes 196616 | tf_op jit(solution)/shard_map/ppermute | solution.py:11
  44.3 192.0 %all-reduce.2.cloned.1.call-start = ((), (), s32[]{:S(2)}) async-start(), calls=%async_computation.2 | async-start | bytes 262144 | tf_op jit(solution)/shard_map/psum | solution.py:91
  44.4 23.4 %copy-start.3 = (bf16[256,256]{1,0:T(8,128)(2,1)S(1)}, bf16[256,256]{1,0:T(8,128)(2,1)}, u32[]{:S(2)}) copy-start(bf16[256,256]{1,0:T(8,128)(2,1)} %param.15) | copy-start | bytes 393220
  44.4 23.3 %copy-start.4 = (f32[256]{0:T(256)S(1)}, f32[256]{0:T(256)}, u32[]{:S(2)}) copy-start(f32[256]{0:T(256)} %param.14) | copy-start | bytes 3076
  44.4 69.3 %copy-start.1 = (s32[128]{0:T(128)S(1)}, s32[128]{0:T(128)}, u32[]{:S(2)}) copy-start(s32[128]{0:T(128)} %get-tuple-element.397) | copy-start | bytes 1540
  44.4 69.3 %copy-start.2 = (s32[128]{0:T(128)S(1)}, s32[128]{0:T(128)}, u32[]{:S(2)}) copy-start(s32[128]{0:T(128)} %get-tuple-element.398) | copy-start | bytes 1540
  131.9 106.0 %collective-permute-start.6 = (f32[256,128]{1,0:T(8,128)S(1)}, f32[256,128]{1,0:T(8,128)S(1)}, u32[]{:S(2)}, u32[]{:S(2)}) collective-permute-start(f32[256,128]{1,0:T(8,128)S(1)} %bitcast.44), channel_id=1, source_target_pairs={{0,2},{2,4},{4,6},{6,8},{8,10},{10,12},{12,14},{14,16},{16,18},{18... | collective-permute-start | bytes 393224 | tf_op jit(solution)/shard_map/ppermute | solution.py:11
  131.9 106.0 %collective-permute-start.5 = (f32[256,128]{1,0:T(8,128)S(1)}, f32[256,128]{1,0:T(8,128)S(1)}, u32[]{:S(2)}, u32[]{:S(2)}) collective-permute-start(f32[256,128]{1,0:T(8,128)S(1)} %bitcast.43), channel_id=1, source_target_pairs={{0,30},{2,0},{4,2},{6,4},{8,6},{10,8},{12,10},{14,12},{16,14},{18,... | collective-permute-start | bytes 393224 | tf_op jit(solution)/shard_map/ppermute | solution.py:11
  137.6 100.4 %collective-permute-start.4 = (f32[256,128]{1,0:T(8,128)S(1)}, f32[256,128]{1,0:T(8,128)S(1)}, u32[]{:S(2)}, u32[]{:S(2)}) collective-permute-start(f32[256,128]{1,0:T(8,128)S(1)} %bitcast.42), channel_id=1, source_target_pairs={{0,28},{2,30},{4,0},{6,2},{8,4},{10,6},{12,8},{14,10},{16,12},{18,... | collective-permute-start | bytes 393224 | tf_op jit(solution)/shard_map/ppermute | solution.py:11
  154.9 83.1 %collective-permute-start.7 = (f32[256,128]{1,0:T(8,128)S(1)}, f32[256,128]{1,0:T(8,128)S(1)}, u32[]{:S(2)}, u32[]{:S(2)}) collective-permute-start(f32[256,128]{1,0:T(8,128)S(1)} %bitcast.41), channel_id=1, source_target_pairs={{0,4},{2,6},{4,8},{6,10},{8,12},{10,14},{12,16},{14,18},{16,20},{1... | collective-permute-start | bytes 393224 | tf_op jit(solution)/shard_map/ppermute | solution.py:11
Sparse Core Ops, SparseCore 0:
  44.5 23.2 reduce-scatter.1
  111.9 124.4 all-reduce.1
where the time goes:
time: 247 us; the launch traced here: 245 us
  waiting for transfers between devices  104 us (42%)
  blocking collectives  42.3 us (17%)
  starting transfers between devices  32 us (13%)
  other arithmetic  24.9 us (10%)
  between operations  14.9 us (6%)
  matrix products  14.4 us (6%)
  local copies, waits for them, and re-layouts  12.6 us (5%)
    psum x1, waiting for transfers between devices, local(): lax.psum((weight_term, bias_term), ('row', 'col'))  81.5 us
    psum x1, blocking collectives, local(): lax.psum((weight_term, bias_term), ('row', 'col'))  40.4 us
    ppermute x8, starting transfers between devices, shifted(): return lax.ppermute(value, axis, pairs)  32 us
    reduce_scatter x1, waiting for transfers between devices, local(): lax.psum_scatter(acc.reshape(dst_tiles * tile, in_width).astype(jnp.bfloa...  16.9 us
    unnamed x15, local copies, waits for them, and re-layouts  7.34 us
    scatter-add x4, other arithmetic, back_step(): return acc_back.at[src_block].add(contrib * live[:, None, None])  6.41 us
    scatter-add x4, other arithmetic, forward_step(): return acc.at[dst_block].add(prod * live[:, None, None])  6.4 us
    ppermute x8, waiting for transfers between devices, shifted(): return lax.ppermute(value, axis, pairs)  5.53 us
  transfers between devices with their start and end apart: 10, of which 3 were waited for; matrix products, arithmetic and copies ran while one was open for 11% of the time, Pallas kernels for 0%

commit v1 on v0

--- a/solution.py
+++ b/solution.py
@@ -88,7 +88,7 @@
         summed, dpre, (((0,), (0,)), ((), ())), preferred_element_type=jnp.float32
     )
     bias_term = jnp.sum(dpre.astype(jnp.float32), 0)
-    weight_total, bias_total = lax.psum((weight_term, bias_term), ("row", "col"))
+    weight_total, bias_total = lax.psum(lax.psum((weight_term, bias_term), "col"), "row")
     scale = math.sqrt(nodes_all)
     grad_weight = weight_total / scale
     grad_bias = bias_total / scale

time: 247 us -> 269 us (1.089)
  waiting for transfers between devices: 104 us -> 130 us
  starting transfers between devices: 32 us -> 24.4 us
  blocking collectives: 42.3 us -> 46.3 us
    psum x1 -> x2, waiting for transfers between devices: 81.5 us -> 100 us  [the longest x1 100 us: local(): lax.psum(lax.psum((weight_term, bias_term), 'col'), 'row')]
    ppermute x8, starting transfers between devices: 32 us -> 24.3 us  [shifted(): return lax.ppermute(value, axis, pairs)]
    ppermute x8, waiting for transfers between devices: 5.53 us -> 12.6 us  [shifted(): return lax.ppermute(value, axis, pairs)]
    psum x1 -> x2, blocking collectives: 40.4 us -> 44.4 us  [the longest x1 41.9 us: local(): lax.psum(lax.psum((weight_term, bias_term), 'col'), 'row')]
  transfers between devices with their start and end apart: 10 -> 11, of which waited for: 3 -> 5; matrix products, arithmetic and copies ran while one was open for 11% -> 10% of each run, Pallas kernels for 0% -> 0%
where the time goes in v1:
time: 269 us; the launch traced here: 267 us
  waiting for transfers between devices  130 us (48%)
  blocking collectives  46.3 us (17%)
  other arithmetic  24.9 us (9%)
  starting transfers between devices  24.4 us (9%)
  between operations  14.6 us (5%)
  matrix products  14.4 us (5%)
  local copies, waits for them, and re-layouts  12.6 us (5%)
    psum x1, waiting for transfers between devices, local(): lax.psum(lax.psum((weight_term, bias_term), 'col'), 'row')  100 us
    psum x1, blocking collectives, local(): lax.psum(lax.psum((weight_term, bias_term), 'col'), 'row')  41.9 us
    ppermute x8, starting transfers between devices, shifted(): return lax.ppermute(value, axis, pairs)  24.3 us
    reduce_scatter x1, waiting for transfers between devices, local(): lax.psum_scatter(acc.reshape(dst_tiles * tile, in_width).astype(jnp.bfloa...  16.9 us
    ppermute x8, waiting for transfers between devices, shifted(): return lax.ppermute(value, axis, pairs)  12.6 us
    unnamed x15, local copies, waits for them, and re-layouts  7.34 us
    scatter-add x4, other arithmetic, back_step(): return acc_back.at[src_block].add(contrib * live[:, None, None])  6.41 us
    scatter-add x4, other arithmetic, forward_step(): return acc.at[dst_block].add(prod * live[:, None, None])  6.4 us
  transfers between devices with their start and end apart: 11, of which 5 were waited for; matrix products, arithmetic and copies ran while one was open for 10% of the time, Pallas kernels for 0%

profile of v1, /device:TPU:0, one launch (start us, length us, event | category | flops | bytes accessed | tf_op | source)
XLA Modules:
  0.0 267.2 jit_solution(3852199006569773221)
XLA Ops:
  7.2 3.0 %collective-permute-start = (bf16[256,128]{1,0:T(8,128)(2,1)}, bf16[256,128]{1,0:T(8,128)(2,1)S(1)}, u32[]{:S(2)}, u32[]{:S(2)}) collective-permute-start(bf16[256,128]{1,0:T(8,128)(2,1)} %param.12), channel_id=1, source_target_pairs={{0,4},{2,6},{4,8},{6,10},{8,12},{10,14},{12,16},{14,18},{16,20},{1... | collective-permute-start | bytes 196616 | tf_op jit(solution)/shard_map/ppermute | solution.py:11
  10.3 4.1 %collective-permute-start.2 = (bf16[256,128]{1,0:T(8,128)(2,1)}, bf16[256,128]{1,0:T(8,128)(2,1)S(1)}, u32[]{:S(2)}, u32[]{:S(2)}) collective-permute-start(bf16[256,128]{1,0:T(8,128)(2,1)} %param.12), channel_id=1, source_target_pairs={{0,30},{2,0},{4,2},{6,4},{8,6},{10,8},{12,10},{14,12},{16,14},{18,... | collective-permute-start | bytes 196616 | tf_op jit(solution)/shard_map/ppermute | solution.py:11
  14.4 1.9 collective-permute-start.3
  17.0 5.5 %collective-permute-done.1 = bf16[256,128]{1,0:T(8,128)(2,1)S(1)} collective-permute-done((bf16[256,128]{1,0:T(8,128)(2,1)}, bf16[256,128]{1,0:T(8,128)(2,1)S(1)}, u32[]{:S(2)}, u32[]{:S(2)}) %collective-permute-start.1) | collective-permute-done | bytes 65568 | tf_op jit(solution)/shard_map/ppermute | solution.py:11
  23.4 20.2 %while.22 = (s32[]{:T(128)}, f32[4,128,128]{2,1,0:T(8,128)S(1)}, s32[]{:T(128)}, s32[128]{0:T(128)}, bf16[128,128,128]{2,1,0:T(8,128)(2,1)}, /*index=5*/s32[128]...) while((s32[]{:T(128)}, f32[4,128,128]{2,1,0:T(8,128)S(1)}, ...), condition=%wide.region_2.3_spmd.clone, body=%wide.region_0.2_spmd.clone.sunk | while | flops 67634328 | bytes 6296307 | solution.py:50
  26.9 1.6 scatter_fusion
  37.0 1.6 scatter_fusion
  44.4 6.4 %copy.12 = bf16[1,128,128,128]{2,3,1,0:T(8,128)(2,1)} copy(bf16[1,128,128,128]{3,2,1,0:T(8,128)(2,1)} %bitcast.38) | data formatting | bytes 8388608 | tf_op args[4]
  50.9 16.9 %reduce-scatter.2.cloned.1.call-done = bf16[256,128]{1,0:T(8,128)(2,1)} async-done(((bf16[512,128]{1,0:T(8,128)(2,1)}), bf16[256,128]{1,0:T(8,128)(2,1)}) %reduce-scatter.2.cloned.1.call-update) | async-done | bytes 65552 | tf_op jit(solution)/shard_map/reduce_scatter | solution.py:51
  67.8 1.8 convert_reduce_fusion
  69.5 2.4 psum.30
  72.0 41.9 %psum.31 = f32[256]{0:T(256)S(1)} all-reduce(f32[256]{0:T(256)S(1)} %psum.30), channel_id=1, replica_groups=mesh['row'=16,'col'=2] {'row'}, use_global_device_ids=true, to_apply=%region_11.12 | all-reduce | flops 256 | bytes 2048 | tf_op jit(solution)/shard_map/psum | solution.py:91
  114.1 1.7 fusion.13
  115.8 1.9 all_gather.3
  117.8 17.5 %while.23 = (s32[]{:T(128)}, f32[10,128,128]{2,1,0:T(8,128)S(1)}, s32[]{:T(128)}, s32[128]{0:T(128)S(1)}, bf16[128,128,128]{1,2,0:T(8,128)(2,1)}, /*index=5*/s32...) while((s32[]{:T(128)}, f32[10,128,128]{2,1,0:T(8,128)S(1)}, ...), condition=%wide.region_6.7_spmd.clone, body=%wide.region_4.6_spmd.clone.sunk | while | flops 67634328 | bytes 6296307 | solution.py:79
  120.6 1.6 scatter_fusion.1
  125.0 1.6 scatter_fusion.1
  129.4 1.6 scatter_fusion.1
  133.7 1.6 scatter_fusion.1
  135.5 5.6 %collective-permute-start.5 = (f32[256,128]{1,0:T(8,128)S(1)}, f32[256,128]{1,0:T(8,128)S(1)}, u32[]{:S(2)}, u32[]{:S(2)}) collective-permute-start(f32[256,128]{1,0:T(8,128)S(1)} %bitcast.43), channel_id=1, source_target_pairs={{0,30},{2,0},{4,2},{6,4},{8,6},{10,8},{12,10},{14,12},{16,14},{18,... | collective-permute-start | bytes 393224 | tf_op jit(solution)/shard_map/ppermute | solution.py:11
  141.1 9.6 %collective-permute-start.4 = (f32[256,128]{1,0:T(8,128)S(1)}, f32[256,128]{1,0:T(8,128)S(1)}, u32[]{:S(2)}, u32[]{:S(2)}) collective-permute-start(f32[256,128]{1,0:T(8,128)S(1)} %bitcast.42), channel_id=1, source_target_pairs={{0,28},{2,30},{4,0},{6,2},{8,4},{10,6},{12,8},{14,10},{16,12},{18,... | collective-permute-start | bytes 393224 | tf_op jit(solution)/shard_map/ppermute | solution.py:11
  151.3 1.9 collective-permute-done.4
  153.2 5.1 %collective-permute-done.7 = f32[256,128]{1,0:T(8,128)S(1)} collective-permute-done((f32[256,128]{1,0:T(8,128)S(1)}, f32[256,128]{1,0:T(8,128)S(1)}, u32[]{:S(2)}, u32[]{:S(2)}) %collective-permute-start.7) | collective-permute-done | bytes 131104 | tf_op jit(solution)/shard_map/ppermute | solution.py:11
  159.0 100.1 %all-reduce.5.cloned.1.call-done = f32[128,256]{1,0:T(8,128)} async-done(((f32[128,256]{1,0:T(8,128)}), f32[128,256]{1,0:T(8,128)}) %all-reduce.5.cloned.1.call-update) | async-done | bytes 131088 | tf_op jit(solution)/shard_map/psum | solution.py:91
  (80 shorter events, 32.6 us)
Async XLA Ops:
  7.2 60.6 %copy-start = (bf16[128,256]{1,0:T(8,128)(2,1)S(1)}, bf16[128,256]{1,0:T(8,128)(2,1)}, u32[]{:S(2)}) copy-start(bf16[128,256]{1,0:T(8,128)(2,1)} %param.13) | copy-start | bytes 196612
  7.2 60.6 %reduce-scatter.2.cloned.1.call-start = ((), (), s32[]{:S(2)}) async-start(), calls=%async_computation.1 | async-start | bytes 196608 | tf_op jit(solution)/shard_map/reduce_scatter | solution.py:51
  7.2 9.7 %collective-permute-start = (bf16[256,128]{1,0:T(8,128)(2,1)}, bf16[256,128]{1,0:T(8,128)(2,1)S(1)}, u32[]{:S(2)}, u32[]{:S(2)}) collective-permute-start(bf16[256,128]{1,0:T(8,128)(2,1)} %param.12), channel_id=1, source_target_pairs={{0,4},{2,6},{4,8},{6,10},{8,12},{10,14},{12,16},{14,18},{16,20},{1... | collective-permute-start | bytes 196616 | tf_op jit(solution)/shard_map/ppermute | solution.py:11
  10.3 13.1 %collective-permute-start.2 = (bf16[256,128]{1,0:T(8,128)(2,1)}, bf16[256,128]{1,0:T(8,128)(2,1)S(1)}, u32[]{:S(2)}, u32[]{:S(2)}) collective-permute-start(bf16[256,128]{1,0:T(8,128)(2,1)} %param.12), channel_id=1, source_target_pairs={{0,30},{2,0},{4,2},{6,4},{8,6},{10,8},{12,10},{14,12},{16,14},{18,... | collective-permute-start | bytes 196616 | tf_op jit(solution)/shard_map/ppermute | solution.py:11
  14.4 8.1 %collective-permute-start.1 = (bf16[256,128]{1,0:T(8,128)(2,1)}, bf16[256,128]{1,0:T(8,128)(2,1)S(1)}, u32[]{:S(2)}, u32[]{:S(2)}) collective-permute-start(bf16[256,128]{1,0:T(8,128)(2,1)} %param.12), channel_id=1, source_target_pairs={{0,2},{2,4},{4,6},{6,8},{8,10},{10,12},{12,14},{14,16},{16,18},{18... | collective-permute-start | bytes 196616 | tf_op jit(solution)/shard_map/ppermute | solution.py:11
  14.4 9.0 %collective-permute-start.3 = (bf16[256,128]{1,0:T(8,128)(2,1)}, bf16[256,128]{1,0:T(8,128)(2,1)S(1)}, u32[]{:S(2)}, u32[]{:S(2)}) collective-permute-start(bf16[256,128]{1,0:T(8,128)(2,1)} %param.12), channel_id=1, source_target_pairs={{0,28},{2,30},{4,0},{6,2},{8,4},{10,6},{12,8},{14,10},{16,12},{18,... | collective-permute-start | bytes 196616 | tf_op jit(solution)/shard_map/ppermute | solution.py:11
  44.3 106.9 %all-reduce.3.cloned.1.call-start = ((), (), s32[]{:S(2)}) async-start(), calls=%async_computation.2 | async-start | bytes 262144 | tf_op jit(solution)/shard_map/psum | solution.py:91
  44.4 23.4 %copy-start.3 = (bf16[256,256]{1,0:T(8,128)(2,1)S(1)}, bf16[256,256]{1,0:T(8,128)(2,1)}, u32[]{:S(2)}) copy-start(bf16[256,256]{1,0:T(8,128)(2,1)} %param.15) | copy-start | bytes 393220
  44.4 23.3 %copy-start.4 = (f32[256]{0:T(256)S(1)}, f32[256]{0:T(256)}, u32[]{:S(2)}) copy-start(f32[256]{0:T(256)} %param.14) | copy-start | bytes 3076
  44.4 73.4 %copy-start.1 = (s32[128]{0:T(128)S(1)}, s32[128]{0:T(128)}, u32[]{:S(2)}) copy-start(s32[128]{0:T(128)} %get-tuple-element.401) | copy-start | bytes 1540
  44.4 73.4 %copy-start.2 = (s32[128]{0:T(128)S(1)}, s32[128]{0:T(128)}, u32[]{:S(2)}) copy-start(s32[128]{0:T(128)} %get-tuple-element.402) | copy-start | bytes 1540
  115.8 143.3 %all-reduce.5.cloned.1.call-start = ((), (), s32[]{:S(2)}) async-start(), calls=%async_computation.3 | async-start | bytes 262144 | tf_op jit(solution)/shard_map/psum | solution.py:91
  135.4 15.9 %collective-permute-start.6 = (f32[256,128]{1,0:T(8,128)S(1)}, f32[256,128]{1,0:T(8,128)S(1)}, u32[]{:S(2)}, u32[]{:S(2)}) collective-permute-start(f32[256,128]{1,0:T(8,128)S(1)} %bitcast.44), channel_id=1, source_target_pairs={{0,2},{2,4},{4,6},{6,8},{8,10},{10,12},{12,14},{14,16},{16,18},{18... | collective-permute-start | bytes 393224 | tf_op jit(solution)/shard_map/ppermute | solution.py:11
  135.5 15.8 %collective-permute-start.5 = (f32[256,128]{1,0:T(8,128)S(1)}, f32[256,128]{1,0:T(8,128)S(1)}, u32[]{:S(2)}, u32[]{:S(2)}) collective-permute-start(f32[256,128]{1,0:T(8,128)S(1)} %bitcast.43), channel_id=1, source_target_pairs={{0,30},{2,0},{4,2},{6,4},{8,6},{10,8},{12,10},{14,12},{16,14},{18,... | collective-permute-start | bytes 393224 | tf_op jit(solution)/shard_map/ppermute | solution.py:11
  141.1 12.1 %collective-permute-start.4 = (f32[256,128]{1,0:T(8,128)S(1)}, f32[256,128]{1,0:T(8,128)S(1)}, u32[]{:S(2)}, u32[]{:S(2)}) collective-permute-start(f32[256,128]{1,0:T(8,128)S(1)} %bitcast.42), channel_id=1, source_target_pairs={{0,28},{2,30},{4,0},{6,2},{8,4},{10,6},{12,8},{14,10},{16,12},{18,... | collective-permute-start | bytes 393224 | tf_op jit(solution)/shard_map/ppermute | solution.py:11
  150.7 7.7 %collective-permute-start.7 = (f32[256,128]{1,0:T(8,128)S(1)}, f32[256,128]{1,0:T(8,128)S(1)}, u32[]{:S(2)}, u32[]{:S(2)}) collective-permute-start(f32[256,128]{1,0:T(8,128)S(1)} %bitcast.41), channel_id=1, source_target_pairs={{0,4},{2,6},{4,8},{6,10},{8,12},{10,14},{12,16},{14,18},{16,20},{1... | collective-permute-start | bytes 393224 | tf_op jit(solution)/shard_map/ppermute | solution.py:11
Sparse Core Ops, SparseCore 0:
  44.5 23.2 reduce-scatter.1
  115.9 13.7 all-reduce.2
  151.4 107.6 all-reduce.4
